TPU v7x, 32 devices: a whole 2x2x4 slice. The times are simulated.
32 devices in a mesh: gx: 16 (over z, y, core), gy: 2 (over x).
Axes of the slice: x: 2, y: 2, z: 4, core: 2. Of those that a mesh axis runs over, the one named last changes fastest.
Arguments:
- state_field: bfloat16 [1, 64, 2048, 2048], P(None, None, 'gx', 'gy'), may hold values from -6 to 6
- spectral_x: bfloat16 [2, 32, 2, 64, 64], P(None, 'gx'), may hold values from -2 to 2
- spectral_y: bfloat16 [2, 32, 2, 64, 64], P(None, 'gy'), may hold values from -2 to 2
- expand_weight: bfloat16 [2, 64, 256], replicated, may hold values from -0.75 to 0.75
- reduce_weight: bfloat16 [2, 256, 64], replicated, may hold values from -0.375 to 0.375
Outputs:
- next_state: bfloat16 [1, 64, 2048, 2048], P(None, None, 'gx', 'gy')
All inputs are finite; a program needn't handle non-finite values.
Results may differ from a plain program's by a relative error of at most 0.025.
Values may be sent and summed in bfloat16 or wider, within the bound.
A program may use at most 128 MiB of HBM per device.

v0:
```python
import jax
import jax.numpy as jnp
from jax import lax
from jax.sharding import PartitionSpec as P

NX = 2048
NY = 2048
MODES = 32
LAYERS = 2


def make_tables(length, modes):
    positions = jnp.arange(length, dtype=jnp.int32)
    orders = jnp.arange(modes, dtype=jnp.int32)
    phase = orders[:, None] * positions[None, :] % length
    angle = 2.0 * jnp.pi * phase.astype(jnp.float32) / length
    factor = 1.0 / jnp.sqrt(jnp.float32(length))
    weight_two = jnp.where(orders == 0, 1.0, 2.0).astype(jnp.float32)[:, None]
    forward = jnp.stack([jnp.cos(angle) * factor, -jnp.sin(angle) * factor], axis=1)
    forward = forward.reshape(2 * modes, length).astype(jnp.bfloat16)
    inverse = jnp.stack(
        [weight_two * jnp.cos(angle) * factor, -weight_two * jnp.sin(angle) * factor], axis=1
    )
    inverse = inverse.reshape(2 * modes, length).T.astype(jnp.bfloat16)
    return (forward, inverse)


def mix_modes(spectrum, weights):
    modes = weights.shape[0]
    shaped = spectrum.reshape((modes, 2) + spectrum.shape[1:])
    real_in, imag_in = (shaped[:, 0], shaped[:, 1])
    real_w, imag_w = (weights[:, 0], weights[:, 1])

    def contract_modes(left, right):
        return jnp.einsum("koi,kzin->kzon", left, right, preferred_element_type=jnp.float32)

    real_out = contract_modes(real_w, real_in) - contract_modes(imag_w, imag_in)
    imag_out = contract_modes(real_w, imag_in) + contract_modes(imag_w, real_in)
    joined = jnp.stack([real_out, imag_out], axis=1).astype(jnp.bfloat16)
    return joined.reshape(spectrum.shape)


def body(state_field, spectral_x, spectral_y, expand_weight, reduce_weight):
    planes, channels, local_rows, local_cols = state_field.shape
    row_first = lax.axis_index("gx") * local_rows
    col_first = lax.axis_index("gy") * local_cols
    forward_x, inverse_x = make_tables(NX, MODES)
    forward_y, inverse_y = make_tables(NY, MODES)
    forward_xloc = lax.dynamic_slice_in_dim(forward_x, row_first, local_rows, 1)
    inverse_xloc = lax.dynamic_slice_in_dim(inverse_x, row_first, local_rows, 0)
    forward_yloc = lax.dynamic_slice_in_dim(forward_y, col_first, local_cols, 1)
    inverse_yloc = lax.dynamic_slice_in_dim(inverse_y, col_first, local_cols, 0)
    state = state_field
    for layer_index in range(LAYERS):
        weights_x = spectral_x[layer_index]
        weights_y = spectral_y[layer_index]
        spec_x = lax.psum_scatter(
            jnp.einsum(
                "kx,zcxy->kzcy", forward_xloc, state, preferred_element_type=jnp.float32
            ).astype(jnp.bfloat16),
            "gx",
            scatter_dimension=0,
            tiled=True,
        )
        spec_y = lax.psum_scatter(
            jnp.einsum(
                "ky,zcxy->kzcx", forward_yloc, state, preferred_element_type=jnp.float32
            ).astype(jnp.bfloat16),
            "gy",
            scatter_dimension=0,
            tiled=True,
        )
        mixed_x = mix_modes(spec_x, weights_x)
        mixed_y = mix_modes(spec_y, weights_y)
        branch_x = jnp.einsum(
            "xk,kzcy->zcxy",
            inverse_xloc,
            lax.all_gather(mixed_x, "gx", axis=0, tiled=True),
            preferred_element_type=jnp.float32,
        ).astype(jnp.bfloat16)
        branch_y = jnp.einsum(
            "yk,kzcx->zcxy",
            inverse_yloc,
            lax.all_gather(mixed_y, "gy", axis=0, tiled=True),
            preferred_element_type=jnp.float32,
        ).astype(jnp.bfloat16)
        total = (branch_x.astype(jnp.float32) + branch_y.astype(jnp.float32)).astype(jnp.bfloat16)
        hidden = jax.nn.gelu(
            jnp.einsum(
                "ch,zcxy->zhxy",
                expand_weight[layer_index],
                total,
                preferred_element_type=jnp.float32,
            ),
            approximate=True,
        )
        hidden = hidden.astype(jnp.bfloat16)
        update = jnp.einsum(
            "hc,zhxy->zcxy", reduce_weight[layer_index], hidden, preferred_element_type=jnp.float32
        )
        state = (state.astype(jnp.float32) + update).astype(jnp.bfloat16)
    return state


def solution(mesh):
    in_specs = (
        P(None, None, "gx", "gy"),
        P(None, "gx", None, None, None),
        P(None, "gy", None, None, None),
        P(),
        P(),
    )
    out_specs = P(None, None, "gx", "gy")
    return jax.shard_map(body, mesh=mesh, in_specs=in_specs, out_specs=out_specs, check_vma=False)
```

profile of v0, /device:TPU:0, one launch (start us, length us, event | category | flops | bytes accessed | tf_op | source)
XLA Modules:
  0.0 755.1 jit_solution(4965803991209931031)
XLA Ops:
  6.5 1.1 multiply_convert_fusion.2
  7.7 0.3 copy.157
  8.0 0.1 convert_element_type.190
  8.1 11.6 %convert_bitcast_fusion.3 = bf16[64,1,64,1024]{3,0,2,1:T(8,128)(2,1)} fusion(bf16[1,64,128,1024]{3,2,1,0:T(8,128)(2,1)} %param.5, bf16[64,2048]{1,0:T(8,128)(2,1)S(1)} %convert_element_type.190, s32[]{:T(128)S(6)} %select_n.57), kind=kOutput, calls=%fused_computation.51 | convolution fusion | flops 1077936128 | bytes 25182212 | tf_op jit(solution)/shard_map/kx,zcxy->kzcy/dot_general | solution.py:58
  19.7 11.4 %copy.158 = bf16[64,1,64,1024]{3,2,1,0:T(8,128)(2,1)} copy(bf16[64,1,64,1024]{3,0,2,1:T(8,128)(2,1)} %convert_bitcast_fusion.3) | data formatting | bytes 16777216 | tf_op jit(solution)/shard_map/convert_element_type | solution.py:60
  31.1 0.0 reduce-scatter.7.cloned.1.call-start
  31.1 9.9 %fusion.60 = bf16[64,1,64,128]{3,0,2,1:T(8,128)(2,1)} fusion(bf16[1,64,128,1024]{3,2,1,0:T(8,128)(2,1)} %param.5, bf16[64,2048]{1,0:T(8,128)(2,1)S(1)} %convert_element_type.190, s32[]{:T(128)S(6)} %select_n.59), kind=kOutput, calls=%fused_computation.54 | convolution fusion | flops 1074266112 | bytes 17956868 | tf_op jit(solution)/shard_map/ky,zcxy->kzcx/dot_general | solution.py:66
  41.1 0.0 all-gather.5.cloned.1.call-start
  41.2 0.6 fusion.148
  41.8 95.6 %reduce-scatter.5.cloned.1.call-done = bf16[4,1,64,1024]{3,2,1,0:T(8,128)(2,1)} async-done(((bf16[64,1,64,1024]{3,2,1,0:T(8,128)(2,1)}), bf16[4,1,64,1024]{3,2,1,0:T(8,128)(2,1)}) %reduce-scatter.5.cloned.1.call-update) | async-done | bytes 524304 | tf_op jit(solution)/shard_map/reduce_scatter | solution.py:57
  137.4 1.2 fusion.90
  138.6 1.2 fusion.81
  139.7 1.2 fusion.91
  140.9 1.2 fusion.80
  142.1 0.1 pad_maximum_fusion
  142.1 0.8 copy.162
  143.0 0.3 all-gather.7.cloned.1.call-start
  143.3 1.0 multiply_convert_fusion.1
  144.2 1.0 multiply_convert_fusion
  145.3 0.3 copy.165
  145.5 0.1 convert_element_type.194
  145.7 1.0 fusion.145
  146.7 13.0 %reduce-scatter.7.cloned.1.call-done = bf16[32,1,64,128]{3,0,2,1:T(8,128)(2,1)} async-done(((bf16[64,1,64,128]{3,0,2,1:T(8,128)(2,1)}), bf16[32,1,64,128]{3,0,2,1:T(8,128)(2,1)}) %reduce-scatter.7.cloned.1.call-update) | async-done | bytes 524304 | tf_op jit(solution)/shard_map/reduce_scatter | solution.py:65
  159.7 2.2 fusion.147
  161.9 0.3 fusion.92
  162.2 0.3 fusion.77
  162.5 0.3 fusion.93
  162.8 0.3 fusion.76
  163.1 0.1 pad_maximum_fusion.1
  163.2 1.2 copy.170
  164.4 0.0 reduce-scatter.9.cloned.1.call-start
  164.4 71.8 %all-gather.5.cloned.1.call-done = bf16[64,1,64,1024]{3,2,1,0:T(8,128)(2,1)} async-done(((bf16[4,1,64,1024]{3,2,1,0:T(8,128)(2,1)}), bf16[64,1,64,1024]{3,2,1,0:T(8,128)(2,1)}) %all-gather.5.cloned.1.call-update) | async-done | bytes 8388624 | tf_op jit(solution)/shard_map/all_gather | solution.py:78
  236.2 15.6 %fusion.46 = bf16[64,1024,128]{2,1,0:T(8,128)(2,1)} fusion(bf16[64,1,64,1024]{3,2,1,0:T(8,128)(2,1)} %all-gather.5.cloned.1.call-done, bf16[64,2048]{1,0:T(8,128)(2,1)S(1)} %convert_element_type.194, s32[]{:T(128)S(6)} %select_n.57), kind=kOutput, calls=%fused_computation.46 | convolution fusion | flops 1073741824 | bytes 25182212 | tf_op jit(solution)/shard_map/xk,kzcy->zcxy/dot_general | solution.py:75
  251.8 5.7 all-gather.7.cloned.1.call-done
  257.5 12.2 %fusion.30 = bf16[64,128,1024]{1,2,0:T(8,128)(2,1)} fusion(bf16[64,1024,128]{2,1,0:T(8,128)(2,1)} %fusion.46, bf16[64,1,64,128]{3,0,2,1:T(8,128)(2,1)} %all-gather.7.cloned.1.call-done, bf16[64,2048]{1,0:T(8,128)(2,1)S(1)} %convert_element_type.194, s32[]{:T(128)S(6)} %select_n.59), kind=kOutput, calls=%fused_computation.34 | convolution fusion | flops 1115684864 | bytes 34734084 | tf_op jit(solution)/shard_map/yk,kzcx->zcxy/dot_general | solution.py:81
  269.7 23.5 %copy.172 = bf16[64,128,1024]{2,0,1:T(8,128)(2,1)} copy(bf16[64,128,1024]{1,2,0:T(8,128)(2,1)} %fusion.30) | data formatting | bytes 33554432 | tf_op jit(solution)/shard_map/reshape.36
  293.2 75.0 %fusion.24 = bf16[1,64,128,1024]{3,1,2,0:T(8,128)(2,1)} fusion(bf16[1,64,128,1024]{3,2,1,0:T(8,128)(2,1)} %param.5, bf16[64,128,1024]{2,0,1:T(8,128)(2,1)} %copy.172, bf16[2,256,64]{1,2,0:T(8,128)(2,1)S(1)} %copy-done.8, bf16[2,64,256]{2,1,0:T(8,128)(2,1)S(1)} %copy-done.9), kind=kOutput, calls=%fused_computation.28 | convolution fusion | flops 8917090304 | bytes 50397184 | tf_op jit(solution)/shard_map/hc,zhxy->zcxy/dot_general | solution.py:98
  368.2 28.9 %convert_bitcast_fusion.2 = bf16[64,1,64,1024]{3,0,2,1:T(8,128)(2,1)} fusion(bf16[64,128,1024]{2,0,1:T(8,128)(2,1)} %bitcast.318, bf16[64,2048]{1,0:T(8,128)(2,1)S(1)} %copy-done.5, s32[]{:T(128)S(6)} %select_n.57), kind=kOutput, calls=%fused_computation.50 | convolution fusion | flops 1077936128 | bytes 25182212 | tf_op jit(solution)/shard_map/kx,zcxy->kzcy/dot_general | solution.py:58
  397.1 11.4 %copy.175 = bf16[64,1,64,1024]{3,2,1,0:T(8,128)(2,1)} copy(bf16[64,1,64,1024]{3,0,2,1:T(8,128)(2,1)} %convert_bitcast_fusion.2) | data formatting | bytes 16777216 | tf_op jit(solution)/shard_map/convert_element_type | solution.py:60
  408.5 0.0 reduce-scatter.11.cloned.1.call-start
  408.6 29.7 %fusion.63 = bf16[64,1,64,128]{3,0,2,1:T(8,128)(2,1)} fusion(bf16[64,128,1024]{2,0,1:T(8,128)(2,1)} %bitcast.319, bf16[64,2048]{1,0:T(8,128)(2,1)S(1)} %copy-done.5, s32[]{:T(128)S(6)} %select_n.59), kind=kOutput, calls=%fused_computation.55 | convolution fusion | flops 1074266112 | bytes 17956868 | tf_op jit(solution)/shard_map/ky,zcxy->kzcx/dot_general | solution.py:66
  438.4 0.0 all-gather.9.cloned.1.call-start
  438.4 73.7 %reduce-scatter.9.cloned.1.call-done = bf16[4,1,64,1024]{3,2,1,0:T(8,128)(2,1)} async-done(((bf16[64,1,64,1024]{3,2,1,0:T(8,128)(2,1)}), bf16[4,1,64,1024]{3,2,1,0:T(8,128)(2,1)}) %reduce-scatter.9.cloned.1.call-update) | async-done | bytes 524304 | tf_op jit(solution)/shard_map/reduce_scatter | solution.py:57
  512.1 1.2 fusion.94
  513.2 1.2 fusion.79
  514.4 1.2 fusion.95
  515.6 1.2 fusion.78
  516.8 0.1 pad_maximum_fusion.2
  516.8 0.8 copy.179
  517.8 16.5 %reduce-scatter.11.cloned.1.call-done = bf16[32,1,64,128]{3,0,2,1:T(8,128)(2,1)} async-done(((bf16[64,1,64,128]{3,0,2,1:T(8,128)(2,1)}), bf16[32,1,64,128]{3,0,2,1:T(8,128)(2,1)}) %reduce-scatter.11.cloned.1.call-update) | async-done | bytes 524304 | tf_op jit(solution)/shard_map/reduce_scatter | solution.py:65
  534.3 2.1 fusion.146
  536.4 0.3 fusion.96
  536.7 0.3 fusion.75
  537.0 0.3 fusion.97
  537.3 0.3 fusion.74
  537.6 0.1 pad_maximum_fusion.3
  537.7 1.1 copy.187
  538.9 71.9 %all-gather.9.cloned.1.call-done = bf16[64,1,64,1024]{3,2,1,0:T(8,128)(2,1)} async-done(((bf16[4,1,64,1024]{3,2,1,0:T(8,128)(2,1)}), bf16[64,1,64,1024]{3,2,1,0:T(8,128)(2,1)}) %all-gather.9.cloned.1.call-update) | async-done | bytes 8388624 | tf_op jit(solution)/shard_map/all_gather | solution.py:78
  610.8 15.5 %fusion.44 = bf16[64,1024,128]{2,1,0:T(8,128)(2,1)} fusion(bf16[64,1,64,1024]{3,2,1,0:T(8,128)(2,1)} %all-gather.9.cloned.1.call-done, bf16[64,2048]{1,0:T(8,128)(2,1)S(1)} %copy-done.2, s32[]{:T(128)S(6)} %select_n.57), kind=kOutput, calls=%fused_computation.44 | convolution fusion | flops 1073741824 | bytes 25182212 | tf_op jit(solution)/shard_map/xk,kzcy->zcxy/dot_general | solution.py:75
  626.2 5.9 all-gather.11.cloned.1.call-done
  632.2 11.8 %fusion.31 = bf16[64,128,1024]{1,2,0:T(8,128)(2,1)} fusion(bf16[64,1024,128]{2,1,0:T(8,128)(2,1)} %fusion.44, bf16[64,1,64,128]{3,0,2,1:T(8,128)(2,1)} %all-gather.11.cloned.1.call-done, bf16[64,2048]{1,0:T(8,128)(2,1)S(1)} %copy-done.2, s32[]{:T(128)S(6)} %select_n.59), kind=kOutput, calls=%fused_computation.35 | convolution fusion | flops 1115684864 | bytes 34734084 | tf_op jit(solution)/shard_map/yk,kzcx->zcxy/dot_general | solution.py:81
  644.0 23.5 %copy.189 = bf16[64,128,1024]{2,0,1:T(8,128)(2,1)} copy(bf16[64,128,1024]{1,2,0:T(8,128)(2,1)} %fusion.31) | data formatting | bytes 33554432 | tf_op jit(solution)/shard_map/reshape.64
  667.5 61.7 %fusion.22 = bf16[1,64,128,1024]{3,1,2,0:T(8,128)(2,1)} fusion(bf16[1,64,128,1024]{3,1,2,0:T(8,128)(2,1)} %fusion.24, bf16[64,128,1024]{2,0,1:T(8,128)(2,1)} %copy.189, bf16[2,256,64]{1,2,0:T(8,128)(2,1)S(1)} %copy-done.8, bf16[2,64,256]{2,1,0:T(8,128)(2,1)S(1)} %copy-done.9), kind=kOutput, calls=%fused_computation.23 | convolution fusion | flops 8917090304 | bytes 50397184 | tf_op jit(solution)/shard_map/hc,zhxy->zcxy/dot_general | solution.py:98
  729.2 18.7 %copy.191 = bf16[1,64,128,1024]{3,2,1,0:T(8,128)(2,1)} copy(bf16[1,64,128,1024]{3,1,2,0:T(8,128)(2,1)} %fusion.22) | data formatting | bytes 33554432 | tf_op jit(solution)/shard_map/convert_element_type | solution.py:101
  (39 shorter events, 0.4 us)
Async XLA Ops:
  6.5 130.9 %reduce-scatter.5.cloned.1.call-start = ((), (), s32[]{:S(2)}) async-start(), calls=%async_computation.4 | async-start | bytes 8912896 | tf_op jit(solution)/shard_map/reduce_scatter | solution.py:57
  8.1 23.1 %copy-start.4 = (bf16[64,2048]{1,0:T(8,128)(2,1)}, bf16[64,2048]{1,0:T(8,128)(2,1)S(1)}, u32[]{:S(2)}) copy-start(bf16[64,2048]{1,0:T(8,128)(2,1)S(1)} %convert_element_type.190) | copy-start | bytes 786436
  31.1 10.1 %copy-start.7 = (bf16[2,2,2,64,64]{4,3,2,1,0:T(8,128)(2,1)S(1)}, bf16[2,2,2,64,64]{4,3,2,1,0:T(8,128)(2,1)}, u32[]{:S(2)}) copy-start(bf16[2,2,2,64,64]{4,3,2,1,0:T(8,128)(2,1)} %param.6) | copy-start | bytes 196612
  31.1 114.6 %copy-start.3 = (bf16[2,16,2,64,64]{4,3,2,1,0:T(8,128)(2,1)S(1)}, bf16[2,16,2,64,64]{4,3,2,1,0:T(8,128)(2,1)}, u32[]{:S(2)}) copy-start(bf16[2,16,2,64,64]{4,3,2,1,0:T(8,128)(2,1)} %param.7) | copy-start | bytes 1572868
  31.1 128.6 %reduce-scatter.7.cloned.1.call-start = ((), (), s32[]{:S(2)}) async-start(), calls=%async_computation.6 | async-start | bytes 1572864 | tf_op jit(solution)/shard_map/reduce_scatter | solution.py:65
  41.1 195.1 %all-gather.5.cloned.1.call-start = ((), (), s32[]{:S(2)}) async-start(), calls=%async_computation.5 | async-start | bytes 8912896 | tf_op jit(solution)/shard_map/all_gather | solution.py:78
  143.0 114.5 %all-gather.7.cloned.1.call-start = ((), (), s32[]{:S(2)}) async-start(), calls=%async_computation.7 | async-start | bytes 1572864 | tf_op jit(solution)/shard_map/all_gather | solution.py:84
  145.7 111.8 %copy-start.1 = (bf16[64,2048]{1,0:T(8,128)(2,1)}, bf16[64,2048]{1,0:T(8,128)(2,1)S(1)}, u32[]{:S(2)}) copy-start(bf16[64,2048]{1,0:T(8,128)(2,1)S(1)} %convert_element_type.194) | copy-start | bytes 786436
  164.4 347.7 %reduce-scatter.9.cloned.1.call-start = ((), (), s32[]{:S(2)}) async-start(), calls=%async_computation.8 | async-start | bytes 8912896 | tf_op jit(solution)/shard_map/reduce_scatter | solution.py:57
  269.7 23.6 %copy-start.8 = (bf16[2,256,64]{1,2,0:T(8,128)(2,1)S(1)}, bf16[2,256,64]{1,2,0:T(8,128)(2,1)}, u32[]{:S(2)}) copy-start(bf16[2,256,64]{1,2,0:T(8,128)(2,1)} %param.9) | copy-start | bytes 196612
  269.7 23.6 %copy-start.9 = (bf16[2,64,256]{2,1,0:T(8,128)(2,1)S(1)}, bf16[2,64,256]{2,1,0:T(8,128)(2,1)}, u32[]{:S(2)}) copy-start(bf16[2,64,256]{2,1,0:T(8,128)(2,1)} %param.8) | copy-start | bytes 196612
  293.2 75.0 %copy-start.5 = (bf16[64,2048]{1,0:T(8,128)(2,1)S(1)}, bf16[64,2048]{1,0:T(8,128)(2,1)}, u32[]{:S(2)}) copy-start(bf16[64,2048]{1,0:T(8,128)(2,1)} %copy-done.4) | copy-start | bytes 786436
  408.5 29.9 %copy-start.6 = (bf16[1,2,2,64,64]{4,3,2,1,0:T(8,128)(2,1)S(1)}, bf16[1,2,2,64,64]{4,3,2,1,0:T(8,128)(2,1)}, u32[]{:S(2)}) copy-start(bf16[1,2,2,64,64]{4,3,2,1,0:T(8,128)(2,1)} %get-tuple-element.11) | copy-start | bytes 98308
  408.5 109.3 %copy-start = (bf16[1,16,2,64,64]{4,3,2,1,0:T(8,128)(2,1)S(1)}, bf16[1,16,2,64,64]{4,3,2,1,0:T(8,128)(2,1)}, u32[]{:S(2)}) copy-start(bf16[1,16,2,64,64]{4,3,2,1,0:T(8,128)(2,1)} %get-tuple-element.5) | copy-start | bytes 786436
  408.5 202.2 %copy-start.2 = (bf16[64,2048]{1,0:T(8,128)(2,1)S(1)}, bf16[64,2048]{1,0:T(8,128)(2,1)}, u32[]{:S(2)}) copy-start(bf16[64,2048]{1,0:T(8,128)(2,1)} %copy-done.1) | copy-start | bytes 786436
  408.5 125.7 %reduce-scatter.11.cloned.1.call-start = ((), (), s32[]{:S(2)}) async-start(), calls=%async_computation.10 | async-start | bytes 1572864 | tf_op jit(solution)/shard_map/reduce_scatter | solution.py:65
  438.4 172.4 %all-gather.9.cloned.1.call-start = ((), (), s32[]{:S(2)}) async-start(), calls=%async_computation.9 | async-start | bytes 8912896 | tf_op jit(solution)/shard_map/all_gather | solution.py:78
  517.7 114.5 %all-gather.11.cloned.1.call-start = ((), (), s32[]{:S(2)}) async-start(), calls=%async_computation.11 | async-start | bytes 1572864 | tf_op jit(solution)/shard_map/all_gather | solution.py:84
Sparse Core Ops, SparseCore 0:
  31.2 106.1 reduce-scatter.4
  139.6 20.0 reduce-scatter.6
  161.9 74.2 all-gather.4
  237.6 19.8 all-gather.6
  408.6 103.4 reduce-scatter.8
  514.2 20.0 reduce-scatter.10
  536.4 74.2 all-gather.8
  612.3 19.8 all-gather.10
where the time goes:
time: 765 us; the launch traced here: 755 us
  waiting for transfers between devices  354 us (46%)
  matrix products  284 us (37%)
  local copies, waits for them, and re-layouts  99.2 us (13%)
  between operations  14.3 us (2%)
    reduce_scatter x2, waiting for transfers between devices, body(): lax.psum_scatter(jnp.einsum('kx,zcxy->kzcy', forward_xloc, state, preferr...  169 us
    all_gather x2, waiting for transfers between devices, body(): lax.all_gather(mixed_x, 'gx', axis=0, tiled=True)  144 us
    dot_general x2, matrix products, body(): jnp.einsum('hc,zhxy->zcxy', reduce_weight[layer_index], hidden, preferred...  137 us
    another operation x2, local copies, waits for them, and re-layouts  47 us
    dot_general x2, matrix products, body(): jnp.einsum('kx,zcxy->kzcy', forward_xloc, state, preferred_element_type=j...  40.5 us
    dot_general x2, matrix products, body(): jnp.einsum('ky,zcxy->kzcx', forward_yloc, state, preferred_element_type=j...  39.7 us
    dot_general x2, matrix products, body(): jnp.einsum('xk,kzcy->zcxy', inverse_xloc, lax.all_gather(mixed_x, 'gx', a...  31.1 us
    reduce_scatter x2, waiting for transfers between devices, body(): lax.psum_scatter(jnp.einsum('ky,zcxy->kzcx', forward_yloc, state, preferr...  29.5 us
  transfers between devices with their start and end apart: 8, of which 8 were waited for; matrix products, arithmetic and copies ran while one was open for 13% of the time, Pallas kernels for 0%

commit v1 on v0

v1 whole, which is shorter than its diff:
```python
import functools

import jax
import jax.numpy as jnp
from jax import lax
from jax.experimental import pallas as pl
from jax.experimental.pallas import tpu as pltpu
from jax.sharding import PartitionSpec as P

CHUNKS = 4
LANES = 128
GELU_A = 0.7978845608028654
GELU_B = 0.044715


def local_tables(first, count, length, modes):
    positions = first + jnp.arange(count, dtype=jnp.int32)
    orders = jnp.arange(modes, dtype=jnp.int32)
    phase = orders[:, None] * positions[None, :] % length
    angle = 2.0 * jnp.pi * phase.astype(jnp.float32) / length
    factor = 1.0 / jnp.sqrt(jnp.float32(length))
    weight_two = jnp.where(orders == 0, 1.0, 2.0).astype(jnp.float32)[:, None]
    real, imag = jnp.cos(angle) * factor, -jnp.sin(angle) * factor
    forward = jnp.stack([real, imag], axis=1).reshape(2 * modes, count)
    inverse = jnp.stack([weight_two * real, weight_two * imag], axis=1)
    inverse = inverse.reshape(2 * modes, count)
    return forward.astype(jnp.bfloat16), inverse.astype(jnp.bfloat16)


def dot(left, right):
    return jnp.dot(left, right, preferred_element_type=jnp.float32)


def group_spectra(base, news, fx, fyt, s_ref, acc_ref):
    rows2 = fx.shape[0]
    count, rows = len(news), news[0].shape[0]
    wide = dot(fx, jnp.concatenate(news, axis=1))
    for i in range(count):
        s_ref[pl.ds((base + i) * rows2, rows2), :] = wide[:, i * LANES : (i + 1) * LANES]
    tall = dot(jnp.concatenate(news, axis=0), fyt)
    for i in range(count):
        acc_ref[base + i] = acc_ref[base + i] + tall[i * rows : (i + 1) * rows]


def write_spectra(specx_ref, specy_ref, s_ref, acc_ref):
    rows2, channels, _ = specx_ref.shape
    for k in range(rows2):
        specx_ref[k] = s_ref[pl.ds(k, channels, stride=rows2), :].astype(jnp.bfloat16)

    @pl.when(pl.program_id(0) == pl.num_programs(0) - 1)
    def _():
        specy_ref[...] = acc_ref[...].astype(jnp.bfloat16)


def clear_first(acc_ref):
    @pl.when(pl.program_id(0) == 0)
    def _():
        acc_ref[...] = jnp.zeros_like(acc_ref)


def first_kernel(state_ref, fx_ref, fyt_ref, specx_ref, specy_ref, s_ref, acc_ref):
    clear_first(acc_ref)
    fx, fyt = fx_ref[...], fyt_ref[...]

    @pl.loop(0, state_ref.shape[0] // 4)
    def _(g):
        base = g * 4
        group_spectra(base, [state_ref[base + i] for i in range(4)], fx, fyt, s_ref, acc_ref)

    write_spectra(specx_ref, specy_ref, s_ref, acc_ref)


def layer_kernel(last, state_ref, mixed_ref, a_ref, iy_ref, w1_ref, w2_ref, *refs):
    if last:
        out_ref, m_ref, t_ref = refs[-3:]
    else:
        fx_ref, fyt_ref, out_ref, specx_ref, specy_ref, m_ref, t_ref, s_ref, acc_ref = refs
        clear_first(acc_ref)
        fx, fyt = fx_ref[...], fyt_ref[...]
    channels, rows, _ = state_ref.shape
    rows2 = mixed_ref.shape[0]
    for k in range(rows2):
        m_ref[pl.ds(k * channels, channels), :] = mixed_ref[k].astype(jnp.float32)
    iy = iy_ref[...]

    @pl.loop(0, channels // 4)
    def _(g):
        for i in range(4):
            c = g * 4 + i
            part = m_ref[pl.ds(c, rows2, stride=channels), :].astype(jnp.bfloat16)
            t_ref[pl.ds(c * rows, rows), :] = dot(a_ref[c], jnp.concatenate([part, iy], axis=0))

    w1, w2 = w1_ref[...], w2_ref[...]
    ca = jnp.bfloat16(GELU_A)
    cb = jnp.bfloat16(GELU_A * GELU_B)

    @pl.loop(0, rows // 8)
    def _(g):
        for j in range(2):
            base = g * 8 + j * 4
            parts = [t_ref[pl.ds(base + i, channels, stride=rows), :] for i in range(4)]
            h = dot(w1, jnp.concatenate(parts, axis=1).astype(jnp.bfloat16)).astype(jnp.bfloat16)
            th = jnp.tanh(h * (ca + cb * (h * h)))
            u = dot(w2, h + h * th)
            for i in range(4):
                t_ref[pl.ds(base + i, channels, stride=rows), :] = u[:, i * LANES : (i + 1) * LANES]

    @pl.loop(0, channels // 4)
    def _(g):
        base = g * 4
        news = []
        for i in range(4):
            c = base + i
            new = state_ref[c].astype(jnp.float32) + t_ref[pl.ds(c * rows, rows), :]
            new = new.astype(jnp.bfloat16)
            out_ref[c] = new
            news.append(new)
        if not last:
            group_spectra(base, news, fx, fyt, s_ref, acc_ref)

    if not last:
        write_spectra(specx_ref, specy_ref, s_ref, acc_ref)


def whole(array):
    zeros = (0,) * array.ndim
    return pl.BlockSpec(array.shape, lambda j: zeros)


def body(state_field, spectral_x, spectral_y, expand_weight, reduce_weight):
    planes, channels, rows, cols = state_field.shape
    layers, hidden = expand_weight.shape[0], expand_weight.shape[2]
    nx, ny = rows * lax.axis_size("gx"), cols * lax.axis_size("gy")
    modes = spectral_x.shape[1] * lax.axis_size("gx")
    rows2 = 2 * modes
    chunks = CHUNKS if cols % (CHUNKS * LANES) == 0 else cols // LANES
    width = cols // chunks
    steps = width // LANES
    forward_x, inverse_x = local_tables(lax.axis_index("gx") * rows, rows, nx, modes)
    forward_y, inverse_y = local_tables(lax.axis_index("gy") * cols, cols, ny, modes)
    forward_yt = forward_y.T
    inverse_xt = inverse_x.T

    def block_matrix(w):
        top = jnp.concatenate([w[..., 0, :, :], -w[..., 1, :, :]], axis=-1)
        low = jnp.concatenate([w[..., 1, :, :], w[..., 0, :, :]], axis=-1)
        return jnp.concatenate([top, low], axis=-2)

    mat_x = block_matrix(spectral_x)
    mat_y = block_matrix(lax.all_gather(spectral_y, "gy", axis=1, tiled=True))

    bf16 = jnp.bfloat16
    s_scr = pltpu.VMEM((channels * rows2, LANES), jnp.float32)
    m_scr = pltpu.VMEM((rows2 * channels, LANES), jnp.float32)
    t_scr = pltpu.VMEM((channels * rows, LANES), jnp.float32)
    acc_scr = pltpu.VMEM((channels, rows, rows2), jnp.float32)
    specx_shape = jax.ShapeDtypeStruct((rows2, channels, width), bf16)
    specx_spec = pl.BlockSpec((rows2, channels, LANES), lambda j: (0, 0, j))
    specy_shape = jax.ShapeDtypeStruct((channels, rows, rows2), bf16)
    specy_spec = pl.BlockSpec((channels, rows, rows2), lambda j: (0, 0, 0))
    params = pltpu.CompilerParams(
        dimension_semantics=("arbitrary",), vmem_limit_bytes=56 * 1024 * 1024
    )
    cells = rows * width

    def cost(flops, moved):
        return pl.CostEstimate(flops=flops, bytes_accessed=moved, transcendentals=0)

    def at(first):
        return pl.BlockSpec((channels, rows, LANES), lambda j: (0, 0, j + first))

    def fyt_spec(first):
        return pl.BlockSpec((LANES, rows2), lambda j: (j + first, 0))

    spectra_flops = 4 * rows2 * channels * cells

    def first_call(state, n):
        return pl.pallas_call(
            first_kernel,
            name="spectra",
            grid=(steps,),
            in_specs=[at(n * steps), whole(forward_x), fyt_spec(n * steps)],
            out_specs=[specx_spec, specy_spec],
            out_shape=[specx_shape, specy_shape],
            scratch_shapes=[s_scr, acc_scr],
            compiler_params=params,
            cost_estimate=cost(spectra_flops, 4 * channels * cells),
        )(state, forward_x, forward_yt)

    def layer_call(last, state, first, n, mixed, a, w1, w2, result):
        ins = [state, mixed, a, inverse_y, w1, w2]
        specs = [
            at(first),
            specx_spec,
            whole(a),
            pl.BlockSpec((rows2, LANES), lambda j: (0, j + n * steps)),
            whole(w1),
            whole(w2),
        ]
        aliases = {}
        scratch = [m_scr, t_scr]
        if last:
            out_shape = [jax.ShapeDtypeStruct((channels, rows, cols), bf16)]
            out_specs = [at(n * steps)]
            if result is not None:
                aliases = {len(ins): 0}
                ins.append(result)
                specs.append(pl.BlockSpec(memory_space=pl.ANY))
        else:
            ins += [forward_x, forward_yt]
            specs += [whole(forward_x), fyt_spec(n * steps)]
            out_shape = [jax.ShapeDtypeStruct((channels, rows, width), bf16), specx_shape, specy_shape]
            out_specs = [at(0), specx_spec, specy_spec]
            scratch += [s_scr, acc_scr]
        flops = (4 * channels * hidden * 2 + 8 * rows2 * channels) * cells
        return pl.pallas_call(
            functools.partial(layer_kernel, last),
            name="layer_last" if last else "layer",
            grid=(steps,),
            in_specs=specs,
            out_specs=out_specs,
            out_shape=out_shape,
            scratch_shapes=scratch,
            input_output_aliases=aliases,
            compiler_params=params,
            cost_estimate=cost(flops, 8 * channels * cells),
        )(*ins)

    state = state_field.reshape(channels, rows, cols)
    pieces = [(state, n * steps) for n in range(chunks)]
    spectra = [first_call(state, n) for n in range(chunks)]
    for layer in range(layers):
        last = layer == layers - 1
        owned = [lax.psum_scatter(s, "gx", scatter_dimension=0, tiled=True) for s, _ in spectra]
        mixed = []
        for part in owned:
            pairs = part.reshape(part.shape[0] // 2, 2 * channels, width)
            product = jnp.einsum(
                "moi,miy->moy", mat_x[layer], pairs, preferred_element_type=jnp.float32
            )
            product = product.astype(bf16).reshape(part.shape)
            mixed.append(lax.all_gather(product, "gx", axis=0, tiled=True))
        spec_y = sum(s.astype(jnp.float32) for _, s in spectra).astype(bf16)
        spec_y = lax.psum(jnp.transpose(spec_y, (2, 0, 1)), "gy")
        mixed_y = jnp.einsum(
            "moi,mix->mox",
            mat_y[layer],
            spec_y.reshape(modes, 2 * channels, rows),
            preferred_element_type=jnp.float32,
        ).astype(bf16)
        mixed_y = jnp.transpose(mixed_y.reshape(rows2, channels, rows), (1, 2, 0))
        a = jnp.concatenate(
            [jnp.broadcast_to(inverse_xt[None], (channels, rows, rows2)), mixed_y], axis=2
        )
        w1 = expand_weight[layer].T
        w2 = (reduce_weight[layer].astype(jnp.float32) * 0.5).astype(bf16).T
        result, next_pieces, next_spectra = None, [], []
        for n in range(chunks):
            source, first = pieces[n]
            outs = layer_call(last, source, first, n, mixed[n], a, w1, w2, result)
            if last:
                result = outs[0]
            else:
                next_pieces.append((outs[0], 0))
                next_spectra.append((outs[1], outs[2]))
        pieces, spectra = next_pieces, next_spectra
    return result.reshape(state_field.shape)


def solution(mesh):
    in_specs = (
        P(None, None, "gx", "gy"),
        P(None, "gx", None, None, None),
        P(None, "gy", None, None, None),
        P(),
        P(),
    )
    out_specs = P(None, None, "gx", "gy")
    return jax.shard_map(body, mesh=mesh, in_specs=in_specs, out_specs=out_specs, check_vma=False)
```

time: 765 us -> 783 us (1.024)
  Pallas kernels: 0 us -> 393 us
  matrix products: 284 us -> 18.2 us
  local copies, waits for them, and re-layouts: 99.2 us -> 18.9 us
  waiting for transfers between devices: 354 us -> 306 us
  other arithmetic: 3.32 us -> 23.1 us
    pallas_call x0 -> x12, Pallas kernels: none -> 393 us  [the longest x8 340 us: layer_call(): pl.pallas_call(functools.partial(layer_kernel, last), name='layer_last' i...]
    dot_general x26 -> x10, matrix products: 284 us -> 18.2 us  [the longest x8 13.9 us: body(): jnp.einsum('moi,miy->moy', mat_x[layer], pairs, preferred_element_type=jn...]
    all_gather x4 -> x9, waiting for transfers between devices: 155 us -> 0.09 us  [the longest x8 0.09 us: body(): mixed.append(lax.all_gather(product, 'gx', axis=0, tiled=True))]
    reduce_scatter x4 -> x8, waiting for transfers between devices: 199 us -> 305 us  [body(): lax.psum_scatter(s, 'gx', scatter_dimension=0, tiled=True)]
    another operation x8 -> x4, local copies, waits for them, and re-layouts: 49.3 us -> 0.91 us  [the longest x2 0.76 us: local_tables(): forward = jnp.stack([real, imag], axis=1).reshape(2 * modes, count)]
    convert_element_type x7 -> x3, local copies, waits for them, and re-layouts: 43.9 us -> 1.64 us  [local_tables(): return (forward.astype(jnp.bfloat16), inverse.astype(jnp.bfloat16))]
    transpose x0 -> x3, other arithmetic: none -> 13.1 us  [the longest x2 12.4 us: body(): spec_y = lax.psum(jnp.transpose(spec_y, (2, 0, 1)), 'gy')]
    concatenate x0 -> x4, other arithmetic: none -> 7.85 us  [the longest x2 6.56 us: body(): jnp.concatenate([jnp.broadcast_to(inverse_xt[None], (channels, rows, rows...]
  transfers between devices with their start and end apart: 8 -> 19, of which waited for: 8 -> 6; matrix products, arithmetic and copies ran while one was open for 13% -> 7% of each run, Pallas kernels for 0% -> 44%
where the time goes in v1:
time: 783 us; the launch traced here: 777 us
  Pallas kernels  393 us (50%)
  waiting for transfers between devices  306 us (39%)
  other arithmetic  23.1 us (3%)
  local copies, waits for them, and re-layouts  18.9 us (2%)
  matrix products  18.2 us (2%)
  between operations  15.9 us (2%)
    pallas_call x8, Pallas kernels, layer_call(): pl.pallas_call(functools.partial(layer_kernel, last), name='layer_last' i...  340 us
    reduce_scatter x8, waiting for transfers between devices, body(): lax.psum_scatter(s, 'gx', scatter_dimension=0, tiled=True)  305 us
    pallas_call x4, Pallas kernels, first_call(): pl.pallas_call(first_kernel, name='spectra', grid=(steps,), in_specs=[at(...  52.9 us
  transfers between devices with their start and end apart: 19, of which 6 were waited for; matrix products, arithmetic and copies ran while one was open for 7% of the time, Pallas kernels for 44%

profile of v1, /device:TPU:0, one launch (start us, length us, event | category | flops | bytes accessed | tf_op | source)
XLA Modules:
  0.0 776.6 jit_solution(11508856935776601382)
XLA Ops:
  7.4 0.1 multiply_convert_fusion.7
  7.5 0.6 copy.40
  8.1 0.6 multiply_convert_fusion.1
  8.7 0.1 copy.41
  8.9 0.1 convert_element_type.141
  8.9 0.9 copy.42
  9.8 13.1 %spectra.5 = (bf16[64,64,256]{2,1,0:T(8,128)(2,1)}, bf16[64,128,64]{2,1,0:T(8,128)(2,1)}) custom-call(bf16[64,128,1024]{2,1,0:T(8,128)(2,1)} %bitcast.91, bf16[64,128]{1,0:T(8,128)(2,1)} %bitcast.121, bf16[1024,64]{1,0:T(8,128)(2,1)} %bitcast.99), custom_call_target="tpu_custom_call" | custom-call | flops 536870912 | bytes 8388608 | tf_op jit(solution)/shard_map/spectra/pallas_call | solution.py:178
  22.9 13.3 %spectra.6 = (bf16[64,64,256]{2,1,0:T(8,128)(2,1)}, bf16[64,128,64]{2,1,0:T(8,128)(2,1)}) custom-call(bf16[64,128,1024]{2,1,0:T(8,128)(2,1)} %bitcast.92, bf16[64,128]{1,0:T(8,128)(2,1)} %bitcast.122, bf16[1024,64]{1,0:T(8,128)(2,1)} %bitcast.100), custom_call_target="tpu_custom_call" | custom-call | flops 536870912 | bytes 8388608 | tf_op jit(solution)/shard_map/spectra/pallas_call | solution.py:178
  36.3 13.2 %spectra.7 = (bf16[64,64,256]{2,1,0:T(8,128)(2,1)}, bf16[64,128,64]{2,1,0:T(8,128)(2,1)}) custom-call(bf16[64,128,1024]{2,1,0:T(8,128)(2,1)} %bitcast.93, bf16[64,128]{1,0:T(8,128)(2,1)} %bitcast.123, bf16[1024,64]{1,0:T(8,128)(2,1)} %bitcast.101), custom_call_target="tpu_custom_call" | custom-call | flops 536870912 | bytes 8388608 | tf_op jit(solution)/shard_map/spectra/pallas_call | solution.py:178
  49.6 13.4 %spectra.4 = (bf16[64,64,256]{2,1,0:T(8,128)(2,1)}, bf16[64,128,64]{2,1,0:T(8,128)(2,1)}) custom-call(bf16[64,128,1024]{2,1,0:T(8,128)(2,1)} %bitcast.94, bf16[64,128]{1,0:T(8,128)(2,1)} %bitcast.124, bf16[1024,64]{1,0:T(8,128)(2,1)} %bitcast.102), custom_call_target="tpu_custom_call" | custom-call | flops 536870912 | bytes 8388608 | tf_op jit(solution)/shard_map/spectra/pallas_call | solution.py:178
  63.0 1.1 copy-done.3
  64.2 1.1 copy.45
  65.3 0.2 all-reduce.3.cloned.1.call-start
  65.5 5.2 fusion
  70.7 2.4 copy.46
  73.3 0.1 maximum_maximum_fusion.1
  73.4 14.3 %reduce-scatter.13.cloned.1.call-done = bf16[4,64,256]{2,1,0:T(8,128)(2,1)} async-done(((bf16[64,64,256]{2,1,0:T(8,128)(2,1)}), bf16[4,64,256]{2,1,0:T(8,128)(2,1)}) %reduce-scatter.13.cloned.1.call-update) | async-done | bytes 131088 | tf_op jit(solution)/shard_map/reduce_scatter | solution.py:234
  87.7 1.7 convolution_convert_fusion.7
  89.5 62.7 %reduce-scatter.15.cloned.1.call-done = bf16[4,64,256]{2,1,0:T(8,128)(2,1)} async-done(((bf16[64,64,256]{2,1,0:T(8,128)(2,1)}), bf16[4,64,256]{2,1,0:T(8,128)(2,1)}) %reduce-scatter.15.cloned.1.call-update) | async-done | bytes 131088 | tf_op jit(solution)/shard_map/reduce_scatter | solution.py:234
  152.2 1.7 convolution_convert_fusion.6
  153.9 0.0 all-gather.20.cloned.1.call-start
  154.0 62.7 %reduce-scatter.17.cloned.1.call-done = bf16[4,64,256]{2,1,0:T(8,128)(2,1)} async-done(((bf16[64,64,256]{2,1,0:T(8,128)(2,1)}), bf16[4,64,256]{2,1,0:T(8,128)(2,1)}) %reduce-scatter.17.cloned.1.call-update) | async-done | bytes 131088 | tf_op jit(solution)/shard_map/reduce_scatter | solution.py:234
  216.7 1.7 convolution_convert_fusion.5
  218.5 65.1 %reduce-scatter.9.cloned.1.call-done = bf16[4,64,256]{2,1,0:T(8,128)(2,1)} async-done(((bf16[64,64,256]{2,1,0:T(8,128)(2,1)}), bf16[4,64,256]{2,1,0:T(8,128)(2,1)}) %reduce-scatter.9.cloned.1.call-update) | async-done | bytes 131088 | tf_op jit(solution)/shard_map/reduce_scatter | solution.py:234
  283.6 1.7 convolution_convert_fusion.9
  285.4 0.1 copy.44
  285.6 0.7 copy.55
  286.3 0.1 copy.48
  286.4 0.7 convert_element_type.150.iy_ref
  287.1 0.6 fusion.10
  287.8 1.5 fusion.20
  289.3 0.4 copy-done.2
  289.7 0.2 slice_bitcast_fusion.4
  289.9 1.2 maximum_maximum_fusion
  291.1 2.4 convolution_convert_fusion.1
  293.5 2.3 copy.47
  295.8 0.5 broadcast_in_dim.14
  296.3 1.1 copy-done.1
  297.4 2.5 pad_maximum_fusion.1.a_ref
  299.9 47.5 %layer.5 = (bf16[64,128,256]{2,1,0:T(8,128)(2,1)}, bf16[64,64,256]{2,1,0:T(8,128)(2,1)}, bf16[64,128,64]{2,1,0:T(8,128)(2,1)}) custom-call(bf16[64,128,1024]{2,1,0:T(8,128)(2,1)} %bitcast.95, bf16[64,64,256]{2,1,0:T(8,128)(2,1)} %all-gather.16.cloned.1.call-done.mixed_ref, bf16[64,128,128]{2,1,0:T(8,128)(2,1)} %pad_maximum_fusion.1.a_ref, ...), custom_call_target="tpu_custom_call" | custom-call | flops 5368709120 | bytes 16777216 | tf_op jit(solution)/shard_map/layer/pallas_call | solution.py:216
  347.4 0.3 reduce-scatter.21.cloned.1.call-start
  347.7 47.5 %layer.6 = (bf16[64,128,256]{2,1,0:T(8,128)(2,1)}, bf16[64,64,256]{2,1,0:T(8,128)(2,1)}, bf16[64,128,64]{2,1,0:T(8,128)(2,1)}) custom-call(bf16[64,128,1024]{2,1,0:T(8,128)(2,1)} %bitcast.96, bf16[64,64,256]{2,1,0:T(8,128)(2,1)} %all-gather.18.cloned.1.call-done.mixed_ref, bf16[64,128,128]{2,1,0:T(8,128)(2,1)} %pad_maximum_fusion.1.a_ref, ...), custom_call_target="tpu_custom_call" | custom-call | flops 5368709120 | bytes 16777216 | tf_op jit(solution)/shard_map/layer/pallas_call | solution.py:216
  395.3 47.5 %layer.7 = (bf16[64,128,256]{2,1,0:T(8,128)(2,1)}, bf16[64,64,256]{2,1,0:T(8,128)(2,1)}, bf16[64,128,64]{2,1,0:T(8,128)(2,1)}) custom-call(bf16[64,128,1024]{2,1,0:T(8,128)(2,1)} %bitcast.97, bf16[64,64,256]{2,1,0:T(8,128)(2,1)} %all-gather.20.cloned.1.call-done.mixed_ref, bf16[64,128,128]{2,1,0:T(8,128)(2,1)} %pad_maximum_fusion.1.a_ref, ...), custom_call_target="tpu_custom_call" | custom-call | flops 5368709120 | bytes 16777216 | tf_op jit(solution)/shard_map/layer/pallas_call | solution.py:216
  443.0 47.6 %layer.4 = (bf16[64,128,256]{2,1,0:T(8,128)(2,1)}, bf16[64,64,256]{2,1,0:T(8,128)(2,1)}, bf16[64,128,64]{2,1,0:T(8,128)(2,1)}) custom-call(bf16[64,128,1024]{2,1,0:T(8,128)(2,1)} %bitcast.98, bf16[64,64,256]{2,1,0:T(8,128)(2,1)} %all-gather.10.cloned.1.call-done.mixed_ref, bf16[64,128,128]{2,1,0:T(8,128)(2,1)} %pad_maximum_fusion.1.a_ref, ...), custom_call_target="tpu_custom_call" | custom-call | flops 5368709120 | bytes 16777216 | tf_op jit(solution)/shard_map/layer/pallas_call | solution.py:216
  490.6 0.0 all-reduce.5.cloned.1.call-start
  490.6 7.2 fusion.1
  497.8 3.5 copy.50
  501.3 0.0 all-gather.26.cloned.1.call-start
  501.4 1.7 convolution_convert_fusion.2
  503.2 1.7 convolution_convert_fusion.3
  505.0 0.0 all-gather.22.cloned.1.call-start
  505.0 32.5 %reduce-scatter.19.cloned.1.call-done = bf16[4,64,256]{2,1,0:T(8,128)(2,1)} async-done(((bf16[64,64,256]{2,1,0:T(8,128)(2,1)}), bf16[4,64,256]{2,1,0:T(8,128)(2,1)}) %reduce-scatter.19.cloned.1.call-update) | async-done | bytes 131088 | tf_op jit(solution)/shard_map/reduce_scatter | solution.py:234
  537.5 1.7 convolution_convert_fusion.4
  539.2 0.3 all-gather.14.cloned.1.call-start
  539.5 67.9 %reduce-scatter.11.cloned.1.call-done = bf16[4,64,256]{2,1,0:T(8,128)(2,1)} async-done(((bf16[64,64,256]{2,1,0:T(8,128)(2,1)}), bf16[4,64,256]{2,1,0:T(8,128)(2,1)}) %reduce-scatter.11.cloned.1.call-update) | async-done | bytes 131088 | tf_op jit(solution)/shard_map/reduce_scatter | solution.py:234
  607.4 1.7 convolution_convert_fusion.8
  609.1 0.7 copy.56
  609.9 2.0 convolution_convert_fusion
  611.9 2.3 copy.51
  614.1 4.1 pad_maximum_fusion.a_ref
  618.2 37.8 %layer_last.4.refs_0_ = bf16[64,128,1024]{2,1,0:T(8,128)(2,1)} custom-call(bf16[64,128,256]{2,1,0:T(8,128)(2,1)} %get-tuple-element.43.state_ref, bf16[64,64,256]{2,1,0:T(8,128)(2,1)} %all-gather.26.cloned.1.call-done.mixed_ref, bf16[64,128,128]{2,1,0:T(8,128)(2,1)} %pad_maximum_fusion.a_ref, bf16[64,1024]{1,0:T(8,128)(2,1)} %convert_element_type.150.iy_ref, ...), custom_call_target="tpu_custom_call" | custom-call | flops 5368709120 | bytes 16777216 | tf_op jit(solution)/shard_map/layer_last/pallas_call | solution.py:216
  656.0 37.5 %layer_last.5.refs_0_ = bf16[64,128,1024]{2,1,0:T(8,128)(2,1)} custom-call(bf16[64,128,256]{2,1,0:T(8,128)(2,1)} %get-tuple-element.41.state_ref, bf16[64,64,256]{2,1,0:T(8,128)(2,1)} %all-gather.24.cloned.1.call-done.mixed_ref, bf16[64,128,128]{2,1,0:T(8,128)(2,1)} %pad_maximum_fusion.a_ref, ...), custom_call_target="tpu_custom_call", output_to_operand_aliasing={{}: (6, {})} | custom-call | flops 5368709120 | bytes 16777216 | tf_op jit(solution)/shard_map/layer_last/pallas_call | solution.py:216
  693.5 37.6 %layer_last.6.refs_0_ = bf16[64,128,1024]{2,1,0:T(8,128)(2,1)} custom-call(bf16[64,128,256]{2,1,0:T(8,128)(2,1)} %get-tuple-element.39.state_ref, bf16[64,64,256]{2,1,0:T(8,128)(2,1)} %all-gather.22.cloned.1.call-done.mixed_ref, bf16[64,128,128]{2,1,0:T(8,128)(2,1)} %pad_maximum_fusion.a_ref, ...), custom_call_target="tpu_custom_call", output_to_operand_aliasing={{}: (6, {})} | custom-call | flops 5368709120 | bytes 16777216 | tf_op jit(solution)/shard_map/layer_last/pallas_call | solution.py:216
  731.0 37.5 %layer_last.7 = bf16[64,128,1024]{2,1,0:T(8,128)(2,1)} custom-call(bf16[64,128,256]{2,1,0:T(8,128)(2,1)} %get-tuple-element.30.state_ref, bf16[64,64,256]{2,1,0:T(8,128)(2,1)} %all-gather.14.cloned.1.call-done.mixed_ref, bf16[64,128,128]{2,1,0:T(8,128)(2,1)} %pad_maximum_fusion.a_ref, ...), custom_call_target="tpu_custom_call", output_to_operand_aliasing={{}: (6, {})} | custom-call | flops 5368709120 | bytes 16777216 | tf_op jit(solution)/shard_map/layer_last/pallas_call | solution.py:216
  (64 shorter events, 1.1 us)
Async XLA Ops:
  7.4 80.3 %reduce-scatter.13.cloned.1.call-start = ((), (), s32[]{:S(2)}) async-start(), calls=%async_computation.14 | async-start | bytes 2228224 | tf_op jit(solution)/shard_map/reduce_scatter | solution.py:234
  22.9 129.3 %reduce-scatter.15.cloned.1.call-start = ((), (), s32[]{:S(2)}) async-start(), calls=%async_computation.16 | async-start | bytes 2228224 | tf_op jit(solution)/shard_map/reduce_scatter | solution.py:234
  36.3 180.4 %reduce-scatter.17.cloned.1.call-start = ((), (), s32[]{:S(2)}) async-start(), calls=%async_computation.18 | async-start | bytes 2228224 | tf_op jit(solution)/shard_map/reduce_scatter | solution.py:234
  49.5 234.1 %reduce-scatter.9.cloned.1.call-start = ((), (), s32[]{:S(2)}) async-start(), calls=%async_computation.8 | async-start | bytes 2228224 | tf_op jit(solution)/shard_map/reduce_scatter | solution.py:234
  62.9 1.2 copy-start.3
  63.0 224.8 %all-gather.12.cloned.1.call-start = ((), (), s32[]{:S(2)}) async-start(), calls=%async_computation.10 | async-start | bytes 3145728 | tf_op jit(solution)/shard_map/all_gather | solution.py:150
  65.3 225.8 %all-reduce.3.cloned.1.call-start = ((), (), s32[]{:S(2)}) async-start(), calls=%async_computation.11 | async-start | bytes 2097152 | tf_op jit(solution)/shard_map/psum | solution.py:244
  70.7 2.5 copy-start.4
  73.1 212.4 %copy-start.5 = (bf16[2,64,256]{2,1,0:T(8,128)(2,1)S(1)}, bf16[2,64,256]{2,1,0:T(8,128)(2,1)}, u32[]{:S(2)}) copy-start(bf16[2,64,256]{2,1,0:T(8,128)(2,1)} %param.8) | copy-start | bytes 196612
  73.1 214.0 %copy-start.6 = (bf16[2,256,64]{1,2,0:T(8,128)(2,1)S(1)}, bf16[2,256,64]{1,2,0:T(8,128)(2,1)}, u32[]{:S(2)}) copy-start(bf16[2,256,64]{1,2,0:T(8,128)(2,1)} %param.9) | copy-start | bytes 196612
  73.2 226.7 %all-gather.16.cloned.1.call-start = ((), (), s32[]{:S(2)}) async-start(), calls=%async_computation.15 | async-start | bytes 2228224 | tf_op jit(solution)/shard_map/all_gather | solution.py:242
  89.4 258.3 %all-gather.18.cloned.1.call-start = ((), (), s32[]{:S(2)}) async-start(), calls=%async_computation.17 | async-start | bytes 2228224 | tf_op jit(solution)/shard_map/all_gather | solution.py:242
  153.9 241.4 %all-gather.20.cloned.1.call-start = ((), (), s32[]{:S(2)}) async-start(), calls=%async_computation.19 | async-start | bytes 2228224 | tf_op jit(solution)/shard_map/all_gather | solution.py:242
  218.5 224.5 %all-gather.10.cloned.1.call-start = ((), (), s32[]{:S(2)}) async-start(), calls=%async_computation.9 | async-start | bytes 2228224 | tf_op jit(solution)/shard_map/all_gather | solution.py:242
  285.4 216.0 %reduce-scatter.23.cloned.1.call-start = ((), (), s32[]{:S(2)}) async-start(), calls=%async_computation.25 | async-start | bytes 2228224 | tf_op jit(solution)/shard_map/reduce_scatter | solution.py:234
  287.8 1.9 copy-start.2
  291.1 2.4 copy-start
  295.8 1.6 copy-start.1
  347.4 155.8 %reduce-scatter.21.cloned.1.call-start = ((), (), s32[]{:S(2)}) async-start(), calls=%async_computation.23 | async-start | bytes 2228224 | tf_op jit(solution)/shard_map/reduce_scatter | solution.py:234
  395.3 142.2 %reduce-scatter.19.cloned.1.call-start = ((), (), s32[]{:S(2)}) async-start(), calls=%async_computation.21 | async-start | bytes 2228224 | tf_op jit(solution)/shard_map/reduce_scatter | solution.py:234
  442.9 164.5 %reduce-scatter.11.cloned.1.call-start = ((), (), s32[]{:S(2)}) async-start(), calls=%async_computation.12 | async-start | bytes 2228224 | tf_op jit(solution)/shard_map/reduce_scatter | solution.py:234
  490.6 119.3 %all-reduce.5.cloned.1.call-start = ((), (), s32[]{:S(2)}) async-start(), calls=%async_computation.20 | async-start | bytes 2097152 | tf_op jit(solution)/shard_map/psum | solution.py:244
  501.3 116.9 %all-gather.26.cloned.1.call-start = ((), (), s32[]{:S(2)}) async-start(), calls=%async_computation.26 | async-start | bytes 2228224 | tf_op jit(solution)/shard_map/all_gather | solution.py:242
  503.1 152.8 %all-gather.24.cloned.1.call-start = ((), (), s32[]{:S(2)}) async-start(), calls=%async_computation.24 | async-start | bytes 2228224 | tf_op jit(solution)/shard_map/all_gather | solution.py:242
  505.0 188.5 %all-gather.22.cloned.1.call-start = ((), (), s32[]{:S(2)}) async-start(), calls=%async_computation.22 | async-start | bytes 2228224 | tf_op jit(solution)/shard_map/all_gather | solution.py:242
  539.2 191.8 %all-gather.14.cloned.1.call-start = ((), (), s32[]{:S(2)}) async-start(), calls=%async_computation.13 | async-start | bytes 2228224 | tf_op jit(solution)/shard_map/all_gather | solution.py:242
Sparse Core Ops, SparseCore 0:
  23.0 64.6 reduce-scatter.12
  91.4 60.7 reduce-scatter.14
  155.9 60.7 reduce-scatter.16
  220.3 63.2 reduce-scatter.8
  347.5 60.7 reduce-scatter.22
  411.9 60.9 reduce-scatter.20
  476.6 60.7 reduce-scatter.18
  541.2 66.1 reduce-scatter.10
Sparse Core Ops, SparseCore 1:
  65.4 35.7 all-gather.11
  103.2 39.9 all-reduce.2
  145.2 41.5 all-gather.15
  188.9 41.1 all-gather.17
  232.3 42.7 all-gather.19
  285.4 40.4 all-gather.9
  501.4 38.9 all-reduce.4
  542.4 42.5 all-gather.25
  587.0 42.7 all-gather.23
  631.9 40.2 all-gather.21
  674.2 40.2 all-gather.13

commit v2 on v1

--- a/solution.py
+++ b/solution.py
@@ -7,7 +7,7 @@
 from jax.experimental.pallas import tpu as pltpu
 from jax.sharding import PartitionSpec as P
 
-CHUNKS = 4
+CHUNKS = 2
 LANES = 128
 GELU_A = 0.7978845608028654
 GELU_B = 0.044715

time: 783 us -> 648 us (0.83)
  waiting for transfers between devices: 306 us -> 217 us
  Pallas kernels: 393 us -> 365 us
    reduce_scatter x8 -> x4, waiting for transfers between devices: 305 us -> 197 us  [body(): lax.psum_scatter(s, 'gx', scatter_dimension=0, tiled=True)]
    all_gather x8 -> x4, waiting for transfers between devices: 0.09 us -> 19.3 us  [body(): mixed.append(lax.all_gather(product, 'gx', axis=0, tiled=True))]
    pallas_call x8 -> x4, Pallas kernels: 340 us -> 321 us  [layer_call(): pl.pallas_call(functools.partial(layer_kernel, last), name='layer_last' i...]
    pallas_call x4 -> x2, Pallas kernels: 52.9 us -> 43.9 us  [first_call(): pl.pallas_call(first_kernel, name='spectra', grid=(steps,), in_specs=[at(...]
  transfers between devices with their start and end apart: 19 -> 11, of which waited for: 6 -> 4; matrix products, arithmetic and copies ran while one was open for 7% -> 7% of each run, Pallas kernels for 44% -> 42%
where the time goes in v2:
time: 648 us; the launch traced here: 647 us
  Pallas kernels  365 us (56%)
  waiting for transfers between devices  217 us (33%)
  local copies, waits for them, and re-layouts  19.1 us (3%)
  other arithmetic  18.4 us (3%)
  between operations  14.9 us (2%)
  matrix products  11.9 us (2%)
    pallas_call x4, Pallas kernels, layer_call(): pl.pallas_call(functools.partial(layer_kernel, last), name='layer_last' i...  321 us
    reduce_scatter x4, waiting for transfers between devices, body(): lax.psum_scatter(s, 'gx', scatter_dimension=0, tiled=True)  197 us
    pallas_call x2, Pallas kernels, first_call(): pl.pallas_call(first_kernel, name='spectra', grid=(steps,), in_specs=[at(...  43.9 us
    all_gather x4, waiting for transfers between devices, body(): mixed.append(lax.all_gather(product, 'gx', axis=0, tiled=True))  19.3 us
  transfers between devices with their start and end apart: 11, of which 4 were waited for; matrix products, arithmetic and copies ran while one was open for 7% of the time, Pallas kernels for 42%

profile of v2, /device:TPU:0, one launch (start us, length us, event | category | flops | bytes accessed | tf_op | source)
XLA Modules:
  0.0 647.1 jit_solution(12769252736048336722)
XLA Ops:
  7.4 0.1 multiply_convert_fusion.7
  7.5 0.6 copy.38
  8.1 0.6 multiply_convert_fusion.1
  8.7 0.1 copy.39
  8.9 0.1 convert_element_type.117
  8.9 0.8 copy.40
  9.8 21.9 %spectra.3 = (bf16[64,64,512]{2,1,0:T(8,128)(2,1)}, bf16[64,128,64]{2,1,0:T(8,128)(2,1)}) custom-call(bf16[64,128,1024]{2,1,0:T(8,128)(2,1)} %bitcast.75, bf16[64,128]{1,0:T(8,128)(2,1)} %bitcast.99, bf16[1024,64]{1,0:T(8,128)(2,1)} %bitcast.85), custom_call_target="tpu_custom_call" | custom-call | flops 1073741824 | bytes 16777216 | tf_op jit(solution)/shard_map/spectra/pallas_call | solution.py:178
  31.7 0.0 reduce-scatter.9.cloned.1.call-update
  31.7 0.0 reduce-scatter.5.cloned.1.call-start
  31.7 21.9 %spectra.2 = (bf16[64,64,512]{2,1,0:T(8,128)(2,1)}, bf16[64,128,64]{2,1,0:T(8,128)(2,1)}) custom-call(bf16[64,128,1024]{2,1,0:T(8,128)(2,1)} %bitcast.76, bf16[64,128]{1,0:T(8,128)(2,1)} %bitcast.100, bf16[1024,64]{1,0:T(8,128)(2,1)} %bitcast.86), custom_call_target="tpu_custom_call" | custom-call | flops 1073741824 | bytes 16777216 | tf_op jit(solution)/shard_map/spectra/pallas_call | solution.py:178
  53.7 0.0 reduce-scatter.5.cloned.1.call-update
  53.7 0.0 all-gather.8.cloned.1.call-start
  53.8 1.2 copy-done.3
  55.0 1.1 copy.43
  56.0 0.0 all-gather.8.cloned.1.call-update
  56.0 0.0 all-reduce.3.cloned.1.call-start
  56.1 3.0 fusion
  59.1 2.5 copy.44
  61.6 0.0 all-reduce.3.cloned.1.call-update
  61.6 0.0 all-gather.12.cloned.1.call-start
  61.7 0.1 maximum_maximum_fusion.1
  61.8 45.6 %reduce-scatter.9.cloned.1.call-done = bf16[4,64,512]{2,1,0:T(8,128)(2,1)} async-done(((bf16[64,64,512]{2,1,0:T(8,128)(2,1)}), bf16[4,64,512]{2,1,0:T(8,128)(2,1)}) %reduce-scatter.9.cloned.1.call-update) | async-done | bytes 262160 | tf_op jit(solution)/shard_map/reduce_scatter | solution.py:234
  107.4 1.9 convolution_convert_fusion.3
  109.3 0.0 all-gather.12.cloned.1.call-update
  109.3 0.0 all-gather.6.cloned.1.call-start
  109.3 86.0 %reduce-scatter.5.cloned.1.call-done = bf16[4,64,512]{2,1,0:T(8,128)(2,1)} async-done(((bf16[64,64,512]{2,1,0:T(8,128)(2,1)}), bf16[4,64,512]{2,1,0:T(8,128)(2,1)}) %reduce-scatter.5.cloned.1.call-update) | async-done | bytes 262160 | tf_op jit(solution)/shard_map/reduce_scatter | solution.py:234
  195.3 1.9 convolution_convert_fusion.5
  197.2 0.2 reduce-scatter.11.cloned.1.call-start
  197.5 0.1 copy.42
  197.6 0.7 copy.53
  198.3 0.1 copy.46
  198.5 0.7 convert_element_type.124.iy_ref
  199.2 0.6 fusion.10
  199.8 1.5 fusion.20
  201.3 0.4 copy-done.2
  201.8 0.2 slice_bitcast_fusion.4
  202.0 1.2 maximum_maximum_fusion
  203.2 0.0 all-reduce.3.cloned.1.call-done
  203.2 2.4 convolution_convert_fusion.1
  205.6 2.3 copy.45
  207.9 0.5 broadcast_in_dim.14
  208.4 1.1 copy-done.1
  209.5 2.5 pad_maximum_fusion.1.a_ref
  211.9 89.4 %layer.3 = (bf16[64,128,512]{2,1,0:T(8,128)(2,1)}, bf16[64,64,512]{2,1,0:T(8,128)(2,1)}, bf16[64,128,64]{2,1,0:T(8,128)(2,1)}) custom-call(bf16[64,128,1024]{2,1,0:T(8,128)(2,1)} %bitcast.77, bf16[64,64,512]{2,1,0:T(8,128)(2,1)} %all-gather.12.cloned.1.call-done.mixed_ref, bf16[64,128,128]{2,1,0:T(8,128)(2,1)} %pad_maximum_fusion.1.a_ref, ...), custom_call_target="tpu_custom_call" | custom-call | flops 10737418240 | bytes 33554432 | tf_op jit(solution)/shard_map/layer/pallas_call | solution.py:216
  301.4 0.0 reduce-scatter.7.cloned.1.call-start
  301.4 0.0 all-gather.6.cloned.1.call-done.mixed_ref
  301.5 89.2 %layer.2 = (bf16[64,128,512]{2,1,0:T(8,128)(2,1)}, bf16[64,64,512]{2,1,0:T(8,128)(2,1)}, bf16[64,128,64]{2,1,0:T(8,128)(2,1)}) custom-call(bf16[64,128,1024]{2,1,0:T(8,128)(2,1)} %bitcast.78, bf16[64,64,512]{2,1,0:T(8,128)(2,1)} %all-gather.6.cloned.1.call-done.mixed_ref, bf16[64,128,128]{2,1,0:T(8,128)(2,1)} %pad_maximum_fusion.1.a_ref, ...), custom_call_target="tpu_custom_call" | custom-call | flops 10737418240 | bytes 33554432 | tf_op jit(solution)/shard_map/layer/pallas_call | solution.py:216
  390.7 0.0 all-reduce.5.cloned.1.call-start
  390.8 4.6 fusion.1
  395.4 3.5 copy.48
  399.0 0.0 all-reduce.5.cloned.1.call-update
  399.0 0.0 all-gather.14.cloned.1.call-start
  399.0 0.0 reduce-scatter.11.cloned.1.call-done
  399.1 1.9 convolution_convert_fusion.2
  401.0 0.3 all-gather.10.cloned.1.call-start
  401.2 65.8 %reduce-scatter.7.cloned.1.call-done = bf16[4,64,512]{2,1,0:T(8,128)(2,1)} async-done(((bf16[64,64,512]{2,1,0:T(8,128)(2,1)}), bf16[4,64,512]{2,1,0:T(8,128)(2,1)}) %reduce-scatter.7.cloned.1.call-update) | async-done | bytes 262160 | tf_op jit(solution)/shard_map/reduce_scatter | solution.py:234
  467.1 1.9 convolution_convert_fusion.4
  469.0 0.7 copy.54
  469.7 2.0 convolution_convert_fusion
  471.7 2.3 copy.49
  473.9 4.1 pad_maximum_fusion.a_ref
  478.1 19.2 %all-gather.14.cloned.1.call-done.mixed_ref = bf16[64,64,512]{2,1,0:T(8,128)(2,1)} async-done(((bf16[4,64,512]{2,1,0:T(8,128)(2,1)}), bf16[64,64,512]{2,1,0:T(8,128)(2,1)}) %all-gather.14.cloned.1.call-update) | async-done | bytes 4194320 | tf_op jit(solution)/shard_map/all_gather | solution.py:242
  497.3 71.3 %layer_last.2.refs_0_ = bf16[64,128,1024]{2,1,0:T(8,128)(2,1)} custom-call(bf16[64,128,512]{2,1,0:T(8,128)(2,1)} %get-tuple-element.23.state_ref, bf16[64,64,512]{2,1,0:T(8,128)(2,1)} %all-gather.14.cloned.1.call-done.mixed_ref, bf16[64,128,128]{2,1,0:T(8,128)(2,1)} %pad_maximum_fusion.a_ref, bf16[64,1024]{1,0:T(8,128)(2,1)} %convert_element_type.124.iy_ref, ...), custom_call_target="tpu_custom_call" | custom-call | flops 10737418240 | bytes 33554432 | tf_op jit(solution)/shard_map/layer_last/pallas_call | solution.py:216
  568.6 71.4 %layer_last.3 = bf16[64,128,1024]{2,1,0:T(8,128)(2,1)} custom-call(bf16[64,128,512]{2,1,0:T(8,128)(2,1)} %get-tuple-element.18.state_ref, bf16[64,64,512]{2,1,0:T(8,128)(2,1)} %all-gather.10.cloned.1.call-done.mixed_ref, bf16[64,128,128]{2,1,0:T(8,128)(2,1)} %pad_maximum_fusion.a_ref, ...), custom_call_target="tpu_custom_call", output_to_operand_aliasing={{}: (6, {})} | custom-call | flops 10737418240 | bytes 33554432 | tf_op jit(solution)/shard_map/layer_last/pallas_call | solution.py:216
  (30 shorter events, 0.2 us)
Async XLA Ops:
  7.4 100.0 %reduce-scatter.9.cloned.1.call-start = ((), (), s32[]{:S(2)}) async-start(), calls=%async_computation.10 | async-start | bytes 4456448 | tf_op jit(solution)/shard_map/reduce_scatter | solution.py:234
  31.7 163.6 %reduce-scatter.5.cloned.1.call-start = ((), (), s32[]{:S(2)}) async-start(), calls=%async_computation.4 | async-start | bytes 4456448 | tf_op jit(solution)/shard_map/reduce_scatter | solution.py:234
  53.7 1.3 copy-start.3
  53.7 146.1 %all-gather.8.cloned.1.call-start = ((), (), s32[]{:S(2)}) async-start(), calls=%async_computation.6 | async-start | bytes 3145728 | tf_op jit(solution)/shard_map/all_gather | solution.py:150
  56.0 147.2 %all-reduce.3.cloned.1.call-start = ((), (), s32[]{:S(2)}) async-start(), calls=%async_computation.7 | async-start | bytes 2097152 | tf_op jit(solution)/shard_map/psum | solution.py:244
  59.1 2.6 copy-start.4
  61.6 136.0 %copy-start.5 = (bf16[2,64,256]{2,1,0:T(8,128)(2,1)S(1)}, bf16[2,64,256]{2,1,0:T(8,128)(2,1)}, u32[]{:S(2)}) copy-start(bf16[2,64,256]{2,1,0:T(8,128)(2,1)} %param.8) | copy-start | bytes 196612
  61.6 137.6 %copy-start.6 = (bf16[2,256,64]{1,2,0:T(8,128)(2,1)S(1)}, bf16[2,256,64]{1,2,0:T(8,128)(2,1)}, u32[]{:S(2)}) copy-start(bf16[2,256,64]{1,2,0:T(8,128)(2,1)} %param.9) | copy-start | bytes 196612
  61.6 150.3 %all-gather.12.cloned.1.call-start = ((), (), s32[]{:S(2)}) async-start(), calls=%async_computation.11 | async-start | bytes 4456448 | tf_op jit(solution)/shard_map/all_gather | solution.py:242
  109.3 192.2 %all-gather.6.cloned.1.call-start = ((), (), s32[]{:S(2)}) async-start(), calls=%async_computation.5 | async-start | bytes 4456448 | tf_op jit(solution)/shard_map/all_gather | solution.py:242
  197.2 201.8 %reduce-scatter.11.cloned.1.call-start = ((), (), s32[]{:S(2)}) async-start(), calls=%async_computation.13 | async-start | bytes 4456448 | tf_op jit(solution)/shard_map/reduce_scatter | solution.py:234
  199.8 2.0 copy-start.2
  203.2 2.4 copy-start
  207.9 1.6 copy-start.1
  301.4 165.7 %reduce-scatter.7.cloned.1.call-start = ((), (), s32[]{:S(2)}) async-start(), calls=%async_computation.8 | async-start | bytes 4456448 | tf_op jit(solution)/shard_map/reduce_scatter | solution.py:234
  390.7 79.0 %all-reduce.5.cloned.1.call-start = ((), (), s32[]{:S(2)}) async-start(), calls=%async_computation.12 | async-start | bytes 2097152 | tf_op jit(solution)/shard_map/psum | solution.py:244
  399.0 98.3 %all-gather.14.cloned.1.call-start = ((), (), s32[]{:S(2)}) async-start(), calls=%async_computation.14 | async-start | bytes 4456448 | tf_op jit(solution)/shard_map/all_gather | solution.py:242
  401.0 167.6 %all-gather.10.cloned.1.call-start = ((), (), s32[]{:S(2)}) async-start(), calls=%async_computation.9 | async-start | bytes 4456448 | tf_op jit(solution)/shard_map/all_gather | solution.py:242
Sparse Core Ops, SparseCore 0:
  31.8 75.5 reduce-scatter.8
  111.2 84.0 reduce-scatter.4
  301.5 72.9 reduce-scatter.10
  390.8 76.1 reduce-scatter.6
Sparse Core Ops, SparseCore 1:
  56.1 35.6 all-gather.7
  94.0 39.9 all-reduce.2
  136.0 65.6 all-gather.11
  203.8 49.9 all-gather.5
  399.1 40.1 all-reduce.4
  441.4 55.8 all-gather.13
  499.3 49.1 all-gather.9
